TPU v7x, 32 devices: a whole 2x2x4 slice. The times are simulated.
32 devices in a mesh: sec: 8 (over y, x, core), ch: 4 (over z).
Axes of the slice: x: 2, y: 2, z: 4, core: 2. Of those that a mesh axis runs over, the one named last changes fastest.
Arguments:
- start_amps: bfloat16 [6, 1024, 2048], P(None, 'ch'), may hold values from -6 to 6
- energies: float32 [6], replicated, may hold values from 0.5 to 2
- thresholds: bfloat16 [8, 1024], P('sec', 'ch'), may hold values from -3 to -1
- intersection: bfloat16 [8, 1024, 1024], P('sec', 'ch'), may hold values from -0.2 to 1
Outputs:
- boundary_amps: bfloat16 [8, 6, 1024, 2048], P('sec', None, 'ch')
All inputs are finite; a program needn't handle non-finite values.
Results may differ from a plain program's by a relative error of at most 0.04.
Values may be sent and summed in bfloat16 or wider, within the bound.
A program may use at most 64 MiB of HBM per device.

v0:
```python
import jax
import jax.numpy as jnp
from jax import lax
from jax.sharding import PartitionSpec as P


def passed_along(value, axis, steps):
    count = lax.axis_size(axis)
    leading, last = (max(0, -steps), min(count, count - steps))
    return lax.ppermute(value, axis, [(source, source + steps) for source in range(leading, last)])


def per_device(start_amps, energies, thresholds, intersection):
    sectors = lax.axis_size("sec")
    sector_index = lax.axis_index("sec")
    groups = lax.axis_size("ch")
    energy_count = energies.shape[0]
    step_count = sectors + energy_count - 1
    row_count = intersection.shape[1]
    width_cols = start_amps.shape[2]
    half_cols = width_cols // 2
    col_width = half_cols // groups
    intersection_whole, thresholds_whole = (
        lax.all_gather(intersection, "ch", axis=1, tiled=True),
        lax.all_gather(thresholds, "ch", axis=1, tiled=True),
    )
    basis_change = intersection_whole[0]
    channel_thresholds = thresholds_whole[0].astype(jnp.float32)
    channel_count = basis_change.shape[0]
    paired = start_amps.reshape(energy_count, row_count, 2, half_cols)
    start_cols = lax.all_to_all(paired, "ch", split_axis=3, concat_axis=1, tiled=True)
    stored_init = jnp.zeros((energy_count, channel_count, 2, col_width), jnp.bfloat16)

    def multiply(flat):
        return jnp.dot(basis_change, flat, preferred_element_type=jnp.float32).astype(jnp.bfloat16)

    def skipped(flat):
        return jnp.zeros((channel_count, 2 * col_width), jnp.bfloat16)

    def step(step_index, state_pair):
        outgoing, stored = state_pair
        incoming = passed_along(outgoing, "sec", 1)
        energy_raw = step_index - sector_index
        active = (energy_raw >= 0) & (energy_raw < energy_count)
        energy_slot = jnp.clip(energy_raw, 0, energy_count - 1)
        initial = lax.dynamic_index_in_dim(start_cols, energy_slot, 0, keepdims=False)
        source = jnp.where(sector_index == 0, initial, incoming).astype(jnp.float32)
        wavenumber = jnp.sqrt(energies[energy_slot] - channel_thresholds)[:, None]
        values_part = source[:, 0, :]
        slopes_part = source[:, 1, :]
        cosine = jnp.cos(wavenumber)
        sine_term = jnp.sin(wavenumber)
        new_values = cosine * values_part + sine_term / wavenumber * slopes_part
        new_slopes = -wavenumber * sine_term * values_part + cosine * slopes_part
        rotated = jnp.stack([new_values, new_slopes], axis=1).astype(jnp.bfloat16)
        flat = rotated.reshape(channel_count, 2 * col_width)
        fresh = lax.cond(active, multiply, skipped, flat)
        fresh = fresh.reshape(channel_count, 2, col_width)
        previous = lax.dynamic_index_in_dim(stored, energy_slot, 0, keepdims=False)
        kept = jnp.where(active, fresh, previous)
        stored = lax.dynamic_update_index_in_dim(stored, kept, energy_slot, 0)
        return (fresh, stored)

    outgoing_init = jnp.zeros((channel_count, 2, col_width), jnp.bfloat16)
    final_pair = lax.fori_loop(0, step_count, step, (outgoing_init, stored_init))
    returned = lax.all_to_all(final_pair[1], "ch", split_axis=1, concat_axis=3, tiled=True)
    return returned.reshape(energy_count, row_count, width_cols)[None]


def solution(mesh):
    in_specs = (P(None, "ch", None), P(), P("sec", "ch"), P("sec", "ch", None))
    out_specs = P("sec", None, "ch", None)
    return jax.shard_map(
        per_device, mesh=mesh, in_specs=in_specs, out_specs=out_specs, check_vma=False
    )
```

profile of v0, /device:TPU:4, one launch (start us, length us, event | category | flops | bytes accessed | tf_op | source)
XLA Modules:
  0.0 743.5 jit_solution(3226323656198132357)
XLA Ops:
  6.5 8.6 %copy.31 = bf16[6,256,2048]{1,2,0:T(8,128)(2,1)} copy(bf16[6,256,2048]{2,1,0:T(8,128)(2,1)} %param.8) | data formatting | bytes 12582912 | tf_op args[0]
  15.1 12.7 %copy.32 = bf16[6,256,2,1024]{1,2,0,3:T(2,128)(2,1)} copy(bf16[6,256,2,1024]{1,3,2,0:T(8,128)(2,1)} %bitcast.29) | data formatting | bytes 12582912 | tf_op jit(solution)/shard_map/reshape | solution.py:30
  27.9 5.4 all-to-all-start
  34.0 140.4 %all_gather.6 = bf16[1,1024]{1,0:T(2,128)(2,1)S(1)} all-gather(bf16[1,256]{1,0:T(2,128)(2,1)S(1)} %copy-done), channel_id=1, replica_groups=mesh['sec'=8,'ch'=4] {'ch'}, dimensions={1}, use_global_device_ids=true | all-gather | bytes 2560 | tf_op jit(solution)/shard_map/all_gather | solution.py:25
  174.4 31.1 %all-to-all-done = bf16[6,256,2,1024]{1,2,0,3:T(2,128)(2,1)} async-done(((bf16[6,256,2,1024]{1,2,0,3:T(2,128)(2,1)}), bf16[6,256,2,1024]{1,2,0,3:T(2,128)(2,1)}, u32[]{:S(2)}, u32[]{:S(2)}) %all-to-all-start) | async-done | bytes 6291488 | tf_op jit(solution)/shard_map/all_to_all | solution.py:31
  205.4 6.4 copy.33
  211.9 8.6 %copy.34 = bf16[6,4,256,2,256]{4,2,1,3,0:T(8,128)(2,1)} copy(bf16[6,4,256,2,256]{2,4,1,3,0:T(8,128)(2,1)} %bitcast.27) | data formatting | bytes 12582912 | tf_op jit(solution)/shard_map/all_to_all | solution.py:31
  221.6 5.9 broadcast_in_dim.14.clone
  227.6 353.1 %while.16 = (s32[]{:T(128)}, bf16[1024,2,256]{0,2,1:T(8,128)(2,1)}, bf16[6,1024,2,256]{3,2,0,1:T(2,128)(2,1)}, s32[]{:T(128)}, f32[6]{0:T(128)S(1)}, /*index=5*/...) while((s32[]{:T(128)}, bf16[1024,2,256]{0,2,1:T(8,128)(2,1)}, ...), condition=%wide.region_3.4_spmd, body=%wide.region_0.3_spmd.sunk | while | flops 1078464512 | bytes 46166332 | solution.py:65
  236.7 10.3 %collective-permute-done = bf16[1024,2,256]{2,0,1:T(8,128)(2,1)S(1)} collective-permute-done((bf16[1024,2,256]{2,0,1:T(8,128)(2,1)}, bf16[1024,2,256]{2,0,1:T(8,128)(2,1)S(1)}, u32[]{:S(2)}, u32[]{:S(2)}) %collective-permute-start) | collective-permute-done | bytes 1048608 | tf_op jit(solution)/shard_map/while/body/eval_jaxpr/ppermute | solution.py:10
  262.2 10.3 %collective-permute-done = bf16[1024,2,256]{2,0,1:T(8,128)(2,1)S(1)} collective-permute-done((bf16[1024,2,256]{2,0,1:T(8,128)(2,1)}, bf16[1024,2,256]{2,0,1:T(8,128)(2,1)S(1)}, u32[]{:S(2)}, u32[]{:S(2)}) %collective-permute-start) | collective-permute-done | bytes 1048608 | tf_op jit(solution)/shard_map/while/body/eval_jaxpr/ppermute | solution.py:10
  287.7 10.3 %collective-permute-done = bf16[1024,2,256]{2,0,1:T(8,128)(2,1)S(1)} collective-permute-done((bf16[1024,2,256]{2,0,1:T(8,128)(2,1)}, bf16[1024,2,256]{2,0,1:T(8,128)(2,1)S(1)}, u32[]{:S(2)}, u32[]{:S(2)}) %collective-permute-start) | collective-permute-done | bytes 1048608 | tf_op jit(solution)/shard_map/while/body/eval_jaxpr/ppermute | solution.py:10
  313.1 10.3 %collective-permute-done = bf16[1024,2,256]{2,0,1:T(8,128)(2,1)S(1)} collective-permute-done((bf16[1024,2,256]{2,0,1:T(8,128)(2,1)}, bf16[1024,2,256]{2,0,1:T(8,128)(2,1)S(1)}, u32[]{:S(2)}, u32[]{:S(2)}) %collective-permute-start) | collective-permute-done | bytes 1048608 | tf_op jit(solution)/shard_map/while/body/eval_jaxpr/ppermute | solution.py:10
  338.6 10.7 %collective-permute-done = bf16[1024,2,256]{2,0,1:T(8,128)(2,1)S(1)} collective-permute-done((bf16[1024,2,256]{2,0,1:T(8,128)(2,1)}, bf16[1024,2,256]{2,0,1:T(8,128)(2,1)S(1)}, u32[]{:S(2)}, u32[]{:S(2)}) %collective-permute-start) | collective-permute-done | bytes 1048608 | tf_op jit(solution)/shard_map/while/body/eval_jaxpr/ppermute | solution.py:10
  351.2 4.9 conditional.2
  368.0 10.3 %collective-permute-done = bf16[1024,2,256]{2,0,1:T(8,128)(2,1)S(1)} collective-permute-done((bf16[1024,2,256]{2,0,1:T(8,128)(2,1)}, bf16[1024,2,256]{2,0,1:T(8,128)(2,1)S(1)}, u32[]{:S(2)}, u32[]{:S(2)}) %collective-permute-start) | collective-permute-done | bytes 1048608 | tf_op jit(solution)/shard_map/while/body/eval_jaxpr/ppermute | solution.py:10
  380.3 4.9 conditional.2
  397.1 10.3 %collective-permute-done = bf16[1024,2,256]{2,0,1:T(8,128)(2,1)S(1)} collective-permute-done((bf16[1024,2,256]{2,0,1:T(8,128)(2,1)}, bf16[1024,2,256]{2,0,1:T(8,128)(2,1)S(1)}, u32[]{:S(2)}, u32[]{:S(2)}) %collective-permute-start) | collective-permute-done | bytes 1048608 | tf_op jit(solution)/shard_map/while/body/eval_jaxpr/ppermute | solution.py:10
  409.4 4.9 conditional.2
  410.7 2.3 convolution_convert_fusion
  426.2 10.3 %collective-permute-done = bf16[1024,2,256]{2,0,1:T(8,128)(2,1)S(1)} collective-permute-done((bf16[1024,2,256]{2,0,1:T(8,128)(2,1)}, bf16[1024,2,256]{2,0,1:T(8,128)(2,1)S(1)}, u32[]{:S(2)}, u32[]{:S(2)}) %collective-permute-start) | collective-permute-done | bytes 1048608 | tf_op jit(solution)/shard_map/while/body/eval_jaxpr/ppermute | solution.py:10
  438.4 4.9 conditional.2
  455.2 10.3 %collective-permute-done = bf16[1024,2,256]{2,0,1:T(8,128)(2,1)S(1)} collective-permute-done((bf16[1024,2,256]{2,0,1:T(8,128)(2,1)}, bf16[1024,2,256]{2,0,1:T(8,128)(2,1)S(1)}, u32[]{:S(2)}, u32[]{:S(2)}) %collective-permute-start) | collective-permute-done | bytes 1048608 | tf_op jit(solution)/shard_map/while/body/eval_jaxpr/ppermute | solution.py:10
  467.5 4.9 conditional.2
  484.3 10.3 %collective-permute-done = bf16[1024,2,256]{2,0,1:T(8,128)(2,1)S(1)} collective-permute-done((bf16[1024,2,256]{2,0,1:T(8,128)(2,1)}, bf16[1024,2,256]{2,0,1:T(8,128)(2,1)S(1)}, u32[]{:S(2)}, u32[]{:S(2)}) %collective-permute-start) | collective-permute-done | bytes 1048608 | tf_op jit(solution)/shard_map/while/body/eval_jaxpr/ppermute | solution.py:10
  496.6 4.9 conditional.2
  513.4 10.3 %collective-permute-done = bf16[1024,2,256]{2,0,1:T(8,128)(2,1)S(1)} collective-permute-done((bf16[1024,2,256]{2,0,1:T(8,128)(2,1)}, bf16[1024,2,256]{2,0,1:T(8,128)(2,1)S(1)}, u32[]{:S(2)}, u32[]{:S(2)}) %collective-permute-start) | collective-permute-done | bytes 1048608 | tf_op jit(solution)/shard_map/while/body/eval_jaxpr/ppermute | solution.py:10
  538.9 10.3 %collective-permute-done = bf16[1024,2,256]{2,0,1:T(8,128)(2,1)S(1)} collective-permute-done((bf16[1024,2,256]{2,0,1:T(8,128)(2,1)}, bf16[1024,2,256]{2,0,1:T(8,128)(2,1)S(1)}, u32[]{:S(2)}, u32[]{:S(2)}) %collective-permute-start) | collective-permute-done | bytes 1048608 | tf_op jit(solution)/shard_map/while/body/eval_jaxpr/ppermute | solution.py:10
  564.3 10.3 %collective-permute-done = bf16[1024,2,256]{2,0,1:T(8,128)(2,1)S(1)} collective-permute-done((bf16[1024,2,256]{2,0,1:T(8,128)(2,1)}, bf16[1024,2,256]{2,0,1:T(8,128)(2,1)S(1)}, u32[]{:S(2)}, u32[]{:S(2)}) %collective-permute-start) | collective-permute-done | bytes 1048608 | tf_op jit(solution)/shard_map/while/body/eval_jaxpr/ppermute | solution.py:10
  580.6 134.3 %all_to_all.33 = bf16[6,1024,2,256]{3,2,0,1:T(2,128)(2,1)S(1)} all-to-all(bf16[6,1024,2,256]{3,2,0,1:T(2,128)(2,1)} %get-tuple-element.205), channel_id=1, replica_groups=mesh['sec'=8,'ch'=4] {'ch'}, dimensions={1} | all-to-all | bytes 12582912 | tf_op jit(solution)/shard_map/all_to_all | solution.py:66
  714.9 10.7 %copy.36 = bf16[6,256,2,4,256]{4,3,2,1,0:T(4,128)(2,1)} copy(bf16[6,256,2,4,256]{4,2,0,1,3:T(2,128)(2,1)S(1)} %bitcast.28) | data formatting | bytes 12582912 | tf_op jit(solution)/shard_map/all_to_all | solution.py:66
  725.6 11.0 %broadcast_in_dim_reshape.3 = bf16[1,6,256,2048]{3,2,1,0:T(8,128)(2,1)} reshape(bf16[6,256,2,4,256]{4,3,2,1,0:T(4,128)(2,1)} %copy.36) | data formatting | bytes 12582912 | tf_op jit(solution)/shard_map/broadcast_in_dim;reshape | solution.py:67
  (235 shorter events, 225.7 us)
Async XLA Ops:
  27.9 6.1 copy-start
  27.9 177.6 %all-to-all-start = ((bf16[6,256,2,1024]{1,2,0,3:T(2,128)(2,1)}), bf16[6,256,2,1024]{1,2,0,3:T(2,128)(2,1)}, u32[]{:S(2)}, u32[]{:S(2)}) async-start(bf16[6,256,2,1024]{1,2,0,3:T(2,128)(2,1)} %copy.32), calls=%async_computation | async-start | bytes 12582912 | tf_op jit(solution)/shard_map/all_to_all | solution.py:31
  33.3 187.2 %all-gather.2.cloned.1.call-start = ((), (), s32[]{:S(2)}) async-start(), calls=%async_computation.2 | async-start | bytes 2621440 | tf_op jit(solution)/shard_map/all_gather | solution.py:24
  220.5 7.1 copy-start.2
  229.8 17.2 %collective-permute-start = (bf16[1024,2,256]{2,0,1:T(8,128)(2,1)}, bf16[1024,2,256]{2,0,1:T(8,128)(2,1)S(1)}, u32[]{:S(2)}, u32[]{:S(2)}) collective-permute-start(bf16[1024,2,256]{2,0,1:T(8,128)(2,1)} %copy.45), channel_id=1, source_target_pairs={{0,4},{4,8},{8,12},{12,16},{16,20},{20,24},{24,28},{1,5},{5,9},{9,... | collective-permute-start | bytes 3145736 | tf_op jit(solution)/shard_map/while/body/eval_jaxpr/ppermute | solution.py:10
  235.8 13.2 %copy-start.1 = (bf16[1024,1024]{1,0:T(8,128)(2,1)S(1)}, bf16[1024,1024]{1,0:T(8,128)(2,1)}, u32[]{:S(2)}) copy-start(bf16[1024,1024]{1,0:T(8,128)(2,1)} %get-tuple-element.365) | copy-start | bytes 6291460 | tf_op jit(solution)/shard_map/while
  255.3 17.2 %collective-permute-start = (bf16[1024,2,256]{2,0,1:T(8,128)(2,1)}, bf16[1024,2,256]{2,0,1:T(8,128)(2,1)S(1)}, u32[]{:S(2)}, u32[]{:S(2)}) collective-permute-start(bf16[1024,2,256]{2,0,1:T(8,128)(2,1)} %copy.45), channel_id=1, source_target_pairs={{0,4},{4,8},{8,12},{12,16},{16,20},{20,24},{24,28},{1,5},{5,9},{9,... | collective-permute-start | bytes 3145736 | tf_op jit(solution)/shard_map/while/body/eval_jaxpr/ppermute | solution.py:10
  261.3 13.2 %copy-start.1 = (bf16[1024,1024]{1,0:T(8,128)(2,1)S(1)}, bf16[1024,1024]{1,0:T(8,128)(2,1)}, u32[]{:S(2)}) copy-start(bf16[1024,1024]{1,0:T(8,128)(2,1)} %get-tuple-element.365) | copy-start | bytes 6291460 | tf_op jit(solution)/shard_map/while
  280.7 17.2 %collective-permute-start = (bf16[1024,2,256]{2,0,1:T(8,128)(2,1)}, bf16[1024,2,256]{2,0,1:T(8,128)(2,1)S(1)}, u32[]{:S(2)}, u32[]{:S(2)}) collective-permute-start(bf16[1024,2,256]{2,0,1:T(8,128)(2,1)} %copy.45), channel_id=1, source_target_pairs={{0,4},{4,8},{8,12},{12,16},{16,20},{20,24},{24,28},{1,5},{5,9},{9,... | collective-permute-start | bytes 3145736 | tf_op jit(solution)/shard_map/while/body/eval_jaxpr/ppermute | solution.py:10
  286.8 13.2 %copy-start.1 = (bf16[1024,1024]{1,0:T(8,128)(2,1)S(1)}, bf16[1024,1024]{1,0:T(8,128)(2,1)}, u32[]{:S(2)}) copy-start(bf16[1024,1024]{1,0:T(8,128)(2,1)} %get-tuple-element.365) | copy-start | bytes 6291460 | tf_op jit(solution)/shard_map/while
  306.2 17.2 %collective-permute-start = (bf16[1024,2,256]{2,0,1:T(8,128)(2,1)}, bf16[1024,2,256]{2,0,1:T(8,128)(2,1)S(1)}, u32[]{:S(2)}, u32[]{:S(2)}) collective-permute-start(bf16[1024,2,256]{2,0,1:T(8,128)(2,1)} %copy.45), channel_id=1, source_target_pairs={{0,4},{4,8},{8,12},{12,16},{16,20},{20,24},{24,28},{1,5},{5,9},{9,... | collective-permute-start | bytes 3145736 | tf_op jit(solution)/shard_map/while/body/eval_jaxpr/ppermute | solution.py:10
  312.2 13.2 %copy-start.1 = (bf16[1024,1024]{1,0:T(8,128)(2,1)S(1)}, bf16[1024,1024]{1,0:T(8,128)(2,1)}, u32[]{:S(2)}) copy-start(bf16[1024,1024]{1,0:T(8,128)(2,1)} %get-tuple-element.365) | copy-start | bytes 6291460 | tf_op jit(solution)/shard_map/while
  331.7 17.6 %collective-permute-start = (bf16[1024,2,256]{2,0,1:T(8,128)(2,1)}, bf16[1024,2,256]{2,0,1:T(8,128)(2,1)S(1)}, u32[]{:S(2)}, u32[]{:S(2)}) collective-permute-start(bf16[1024,2,256]{2,0,1:T(8,128)(2,1)} %copy.45), channel_id=1, source_target_pairs={{0,4},{4,8},{8,12},{12,16},{16,20},{20,24},{24,28},{1,5},{5,9},{9,... | collective-permute-start | bytes 3145736 | tf_op jit(solution)/shard_map/while/body/eval_jaxpr/ppermute | solution.py:10
  337.7 13.5 %copy-start.1 = (bf16[1024,1024]{1,0:T(8,128)(2,1)S(1)}, bf16[1024,1024]{1,0:T(8,128)(2,1)}, u32[]{:S(2)}) copy-start(bf16[1024,1024]{1,0:T(8,128)(2,1)} %get-tuple-element.365) | copy-start | bytes 6291460 | tf_op jit(solution)/shard_map/while
  361.1 17.2 %collective-permute-start = (bf16[1024,2,256]{2,0,1:T(8,128)(2,1)}, bf16[1024,2,256]{2,0,1:T(8,128)(2,1)S(1)}, u32[]{:S(2)}, u32[]{:S(2)}) collective-permute-start(bf16[1024,2,256]{2,0,1:T(8,128)(2,1)} %copy.45), channel_id=1, source_target_pairs={{0,4},{4,8},{8,12},{12,16},{16,20},{20,24},{24,28},{1,5},{5,9},{9,... | collective-permute-start | bytes 3145736 | tf_op jit(solution)/shard_map/while/body/eval_jaxpr/ppermute | solution.py:10
  367.1 13.2 %copy-start.1 = (bf16[1024,1024]{1,0:T(8,128)(2,1)S(1)}, bf16[1024,1024]{1,0:T(8,128)(2,1)}, u32[]{:S(2)}) copy-start(bf16[1024,1024]{1,0:T(8,128)(2,1)} %get-tuple-element.365) | copy-start | bytes 6291460 | tf_op jit(solution)/shard_map/while
  390.2 17.2 %collective-permute-start = (bf16[1024,2,256]{2,0,1:T(8,128)(2,1)}, bf16[1024,2,256]{2,0,1:T(8,128)(2,1)S(1)}, u32[]{:S(2)}, u32[]{:S(2)}) collective-permute-start(bf16[1024,2,256]{2,0,1:T(8,128)(2,1)} %copy.45), channel_id=1, source_target_pairs={{0,4},{4,8},{8,12},{12,16},{16,20},{20,24},{24,28},{1,5},{5,9},{9,... | collective-permute-start | bytes 3145736 | tf_op jit(solution)/shard_map/while/body/eval_jaxpr/ppermute | solution.py:10
  396.2 13.2 %copy-start.1 = (bf16[1024,1024]{1,0:T(8,128)(2,1)S(1)}, bf16[1024,1024]{1,0:T(8,128)(2,1)}, u32[]{:S(2)}) copy-start(bf16[1024,1024]{1,0:T(8,128)(2,1)} %get-tuple-element.365) | copy-start | bytes 6291460 | tf_op jit(solution)/shard_map/while
  419.3 17.2 %collective-permute-start = (bf16[1024,2,256]{2,0,1:T(8,128)(2,1)}, bf16[1024,2,256]{2,0,1:T(8,128)(2,1)S(1)}, u32[]{:S(2)}, u32[]{:S(2)}) collective-permute-start(bf16[1024,2,256]{2,0,1:T(8,128)(2,1)} %copy.45), channel_id=1, source_target_pairs={{0,4},{4,8},{8,12},{12,16},{16,20},{20,24},{24,28},{1,5},{5,9},{9,... | collective-permute-start | bytes 3145736 | tf_op jit(solution)/shard_map/while/body/eval_jaxpr/ppermute | solution.py:10
  425.3 13.2 %copy-start.1 = (bf16[1024,1024]{1,0:T(8,128)(2,1)S(1)}, bf16[1024,1024]{1,0:T(8,128)(2,1)}, u32[]{:S(2)}) copy-start(bf16[1024,1024]{1,0:T(8,128)(2,1)} %get-tuple-element.365) | copy-start | bytes 6291460 | tf_op jit(solution)/shard_map/while
  448.3 17.2 %collective-permute-start = (bf16[1024,2,256]{2,0,1:T(8,128)(2,1)}, bf16[1024,2,256]{2,0,1:T(8,128)(2,1)S(1)}, u32[]{:S(2)}, u32[]{:S(2)}) collective-permute-start(bf16[1024,2,256]{2,0,1:T(8,128)(2,1)} %copy.45), channel_id=1, source_target_pairs={{0,4},{4,8},{8,12},{12,16},{16,20},{20,24},{24,28},{1,5},{5,9},{9,... | collective-permute-start | bytes 3145736 | tf_op jit(solution)/shard_map/while/body/eval_jaxpr/ppermute | solution.py:10
  454.4 13.2 %copy-start.1 = (bf16[1024,1024]{1,0:T(8,128)(2,1)S(1)}, bf16[1024,1024]{1,0:T(8,128)(2,1)}, u32[]{:S(2)}) copy-start(bf16[1024,1024]{1,0:T(8,128)(2,1)} %get-tuple-element.365) | copy-start | bytes 6291460 | tf_op jit(solution)/shard_map/while
  477.4 17.2 %collective-permute-start = (bf16[1024,2,256]{2,0,1:T(8,128)(2,1)}, bf16[1024,2,256]{2,0,1:T(8,128)(2,1)S(1)}, u32[]{:S(2)}, u32[]{:S(2)}) collective-permute-start(bf16[1024,2,256]{2,0,1:T(8,128)(2,1)} %copy.45), channel_id=1, source_target_pairs={{0,4},{4,8},{8,12},{12,16},{16,20},{20,24},{24,28},{1,5},{5,9},{9,... | collective-permute-start | bytes 3145736 | tf_op jit(solution)/shard_map/while/body/eval_jaxpr/ppermute | solution.py:10
  483.4 13.2 %copy-start.1 = (bf16[1024,1024]{1,0:T(8,128)(2,1)S(1)}, bf16[1024,1024]{1,0:T(8,128)(2,1)}, u32[]{:S(2)}) copy-start(bf16[1024,1024]{1,0:T(8,128)(2,1)} %get-tuple-element.365) | copy-start | bytes 6291460 | tf_op jit(solution)/shard_map/while
  506.5 17.2 %collective-permute-start = (bf16[1024,2,256]{2,0,1:T(8,128)(2,1)}, bf16[1024,2,256]{2,0,1:T(8,128)(2,1)S(1)}, u32[]{:S(2)}, u32[]{:S(2)}) collective-permute-start(bf16[1024,2,256]{2,0,1:T(8,128)(2,1)} %copy.45), channel_id=1, source_target_pairs={{0,4},{4,8},{8,12},{12,16},{16,20},{20,24},{24,28},{1,5},{5,9},{9,... | collective-permute-start | bytes 3145736 | tf_op jit(solution)/shard_map/while/body/eval_jaxpr/ppermute | solution.py:10
  512.5 13.2 %copy-start.1 = (bf16[1024,1024]{1,0:T(8,128)(2,1)S(1)}, bf16[1024,1024]{1,0:T(8,128)(2,1)}, u32[]{:S(2)}) copy-start(bf16[1024,1024]{1,0:T(8,128)(2,1)} %get-tuple-element.365) | copy-start | bytes 6291460 | tf_op jit(solution)/shard_map/while
  532.0 17.2 %collective-permute-start = (bf16[1024,2,256]{2,0,1:T(8,128)(2,1)}, bf16[1024,2,256]{2,0,1:T(8,128)(2,1)S(1)}, u32[]{:S(2)}, u32[]{:S(2)}) collective-permute-start(bf16[1024,2,256]{2,0,1:T(8,128)(2,1)} %copy.45), channel_id=1, source_target_pairs={{0,4},{4,8},{8,12},{12,16},{16,20},{20,24},{24,28},{1,5},{5,9},{9,... | collective-permute-start | bytes 3145736 | tf_op jit(solution)/shard_map/while/body/eval_jaxpr/ppermute | solution.py:10
  538.0 13.2 %copy-start.1 = (bf16[1024,1024]{1,0:T(8,128)(2,1)S(1)}, bf16[1024,1024]{1,0:T(8,128)(2,1)}, u32[]{:S(2)}) copy-start(bf16[1024,1024]{1,0:T(8,128)(2,1)} %get-tuple-element.365) | copy-start | bytes 6291460 | tf_op jit(solution)/shard_map/while
  557.4 17.2 %collective-permute-start = (bf16[1024,2,256]{2,0,1:T(8,128)(2,1)}, bf16[1024,2,256]{2,0,1:T(8,128)(2,1)S(1)}, u32[]{:S(2)}, u32[]{:S(2)}) collective-permute-start(bf16[1024,2,256]{2,0,1:T(8,128)(2,1)} %copy.45), channel_id=1, source_target_pairs={{0,4},{4,8},{8,12},{12,16},{16,20},{20,24},{24,28},{1,5},{5,9},{9,... | collective-permute-start | bytes 3145736 | tf_op jit(solution)/shard_map/while/body/eval_jaxpr/ppermute | solution.py:10
  563.4 13.2 %copy-start.1 = (bf16[1024,1024]{1,0:T(8,128)(2,1)S(1)}, bf16[1024,1024]{1,0:T(8,128)(2,1)}, u32[]{:S(2)}) copy-start(bf16[1024,1024]{1,0:T(8,128)(2,1)} %get-tuple-element.365) | copy-start | bytes 6291460 | tf_op jit(solution)/shard_map/while
Sparse Core Ops, SparseCore 0:
  35.6 86.7 all-gather.1
where the time goes:
time: 746 us; the launch traced here: 744 us
  blocking collectives  275 us (37%)
  local copies, waits for them, and re-layouts  206 us (28%)
  waiting for transfers between devices  166 us (22%)
  other arithmetic  38.1 us (5%)
  starting transfers between devices  30.2 us (4%)
  matrix products  13.9 us (2%)
  between operations  13.4 us (2%)
    all_gather x1, blocking collectives, per_device(): lax.all_gather(thresholds, 'ch', axis=1, tiled=True)  140 us
    ppermute x13, waiting for transfers between devices, passed_along(): lax.ppermute(value, axis, [(source, source + steps) for source in range(l...  134 us
    all_to_all x1, blocking collectives, per_device(): lax.all_to_all(final_pair[1], 'ch', split_axis=1, concat_axis=3, tiled=True)  134 us
    dynamic_slice x26, local copies, waits for them, and re-layouts, step(): previous = lax.dynamic_index_in_dim(stored, energy_slot, 0, keepdims=False)  44.3 us
    dynamic_update_slice x26, local copies, waits for them, and re-layouts, step(): stored = lax.dynamic_update_index_in_dim(stored, kept, energy_slot, 0)  34.2 us
    all_to_all x1, waiting for transfers between devices, per_device(): lax.all_to_all(paired, 'ch', split_axis=3, concat_axis=1, tiled=True)  31.1 us
    another operation x13, local copies, waits for them, and re-layouts  29.2 us
    ppermute x13, starting transfers between devices, passed_along(): lax.ppermute(value, axis, [(source, source + steps) for source in range(l...  24.8 us
  transfers between devices with their start and end apart: 15, of which 14 were waited for; matrix products, arithmetic and copies ran while one was open for 11% of the time, Pallas kernels for 0%

commit v1 on v0

--- a/solution.py
+++ b/solution.py
@@ -28,7 +28,10 @@
     channel_thresholds = thresholds_whole[0].astype(jnp.float32)
     channel_count = basis_change.shape[0]
     paired = start_amps.reshape(energy_count, row_count, 2, half_cols)
-    start_cols = lax.all_to_all(paired, "ch", split_axis=3, concat_axis=1, tiled=True)
+    start_cols = jnp.concatenate(
+        lax.all_to_all(jnp.stack(jnp.split(paired, lax.axis_size("ch"), axis=3)), "ch", 0, 0),
+        axis=1,
+    )
     stored_init = jnp.zeros((energy_count, channel_count, 2, col_width), jnp.bfloat16)
 
     def multiply(flat):

time: 746 us -> 746 us (level)
  local copies, waits for them, and re-layouts: 206 us -> 192 us
  other arithmetic: 38.1 us -> 48.7 us
    another operation x0 -> x1, other arithmetic: none -> 12.5 us  [per_device(): jnp.stack(jnp.split(paired, lax.axis_size('ch'), axis=3))]
    unnamed x5 -> x4, local copies, waits for them, and re-layouts: 8.61 us -> 0.01 us
    all_to_all x2 -> x1, local copies, waits for them, and re-layouts: 15 us -> 6.63 us  [per_device(): lax.all_to_all(jnp.stack(jnp.split(paired, lax.axis_size('ch'), axis=3)),...]
    another operation x13 -> x14, local copies, waits for them, and re-layouts: 29.2 us -> 35.3 us
  transfers between devices with their start and end apart: 15 -> 15, of which waited for: 14 -> 14; matrix products, arithmetic and copies ran while one was open for 11% -> 9% of each run, Pallas kernels for 0% -> 0%
where the time goes in v1:
time: 746 us; the launch traced here: 744 us
  blocking collectives  275 us (37%)
  local copies, waits for them, and re-layouts  192 us (26%)
  waiting for transfers between devices  169 us (23%)
  other arithmetic  48.7 us (7%)
  starting transfers between devices  30.2 us (4%)
  matrix products  13.9 us (2%)
  between operations  13.4 us (2%)
    all_gather x1, blocking collectives, per_device(): lax.all_gather(thresholds, 'ch', axis=1, tiled=True)  140 us
    ppermute x13, waiting for transfers between devices, passed_along(): lax.ppermute(value, axis, [(source, source + steps) for source in range(l...  138 us
    all_to_all x1, blocking collectives, per_device(): lax.all_to_all(final_pair[1], 'ch', split_axis=1, concat_axis=3, tiled=True)  134 us
    dynamic_slice x26, local copies, waits for them, and re-layouts, step(): previous = lax.dynamic_index_in_dim(stored, energy_slot, 0, keepdims=False)  44.3 us
    dynamic_update_slice x26, local copies, waits for them, and re-layouts, step(): stored = lax.dynamic_update_index_in_dim(stored, kept, energy_slot, 0)  34.2 us
    all_to_all x1, waiting for transfers between devices, per_device(): lax.all_to_all(jnp.stack(jnp.split(paired, lax.axis_size('ch'), axis=3)),...  31.1 us
    another operation x13, local copies, waits for them, and re-layouts  29.4 us
    ppermute x13, starting transfers between devices, passed_along(): lax.ppermute(value, axis, [(source, source + steps) for source in range(l...  24.8 us
  transfers between devices with their start and end apart: 15, of which 14 were waited for; matrix products, arithmetic and copies ran while one was open for 9% of the time, Pallas kernels for 0%

profile of v1, /device:TPU:4, one launch (start us, length us, event | category | flops | bytes accessed | tf_op | source)
XLA Modules:
  0.0 743.5 jit_solution(12281299105284059435)
XLA Ops:
  6.5 11.1 %reshape.111 = bf16[6,256,2,1024]{3,2,1,0:T(2,128)(2,1)} reshape(bf16[6,256,2048]{2,1,0:T(8,128)(2,1)} %param.8) | data formatting | bytes 12582912 | tf_op jit(solution)/shard_map/reshape | solution.py:30
  17.6 5.9 slice_bitcast_fusion.3
  23.6 12.5 %pad_maximum_fusion.1 = bf16[4,6,256,2,256]{4,3,2,1,0:T(2,128)(2,1)} fusion(bf16[1,6,256,2,256]{4,3,2,1,0:T(2,128)(2,1)S(1)} %get-tuple-element.241, bf16[1,6,256,2,256]{4,3,2,1,0:T(2,128)(2,1)S(1)} %get-tuple-element.242, bf16[1,6,256,2,256]{4,3,2,1,0:T(2,128)(2,1)S(1)} %get-tuple-element.243, bf16[1,6,256,2,256]{4,3,2,1,0:T(2,128)(2,1)S(1)} %get-tuple-element.240), kind=kLoop, calls=%fused_computation.14 | loop fusion | flops 9437184 | bytes 12582912 | tf_op jit(solution)/shard_map/stack | solution.py:32
  36.1 5.4 all-to-all-start
  42.2 140.4 %all_gather.6 = bf16[1,1024]{1,0:T(2,128)(2,1)S(1)} all-gather(bf16[1,256]{1,0:T(2,128)(2,1)S(1)} %copy-done), channel_id=1, replica_groups=mesh['sec'=8,'ch'=4] {'ch'}, dimensions={1}, use_global_device_ids=true | all-gather | bytes 2560 | tf_op jit(solution)/shard_map/all_gather | solution.py:25
  182.6 31.1 %all-to-all-done = bf16[4,6,256,2,256]{4,3,2,1,0:T(2,128)(2,1)} async-done(((bf16[4,6,256,2,256]{4,3,2,1,0:T(2,128)(2,1)}), bf16[4,6,256,2,256]{4,3,2,1,0:T(2,128)(2,1)}, u32[]{:S(2)}, u32[]{:S(2)}) %all-to-all-start) | async-done | bytes 6291488 | tf_op jit(solution)/shard_map/all_to_all | solution.py:32
  213.6 6.6 copy.20
  221.4 5.9 broadcast_in_dim.14.clone
  227.3 353.3 %while.16 = (s32[]{:T(128)}, bf16[1024,2,256]{0,2,1:T(8,128)(2,1)}, bf16[6,1024,2,256]{3,2,0,1:T(2,128)(2,1)}, s32[]{:T(128)}, f32[6]{0:T(128)S(1)}, /*index=5*/...) while((s32[]{:T(128)}, bf16[1024,2,256]{0,2,1:T(8,128)(2,1)}, ...), condition=%wide.region_3.4_spmd, body=%wide.region_0.3_spmd.sunk | while | flops 1078464512 | bytes 46166332 | solution.py:68
  236.3 10.6 %collective-permute-done = bf16[1024,2,256]{2,0,1:T(8,128)(2,1)S(1)} collective-permute-done((bf16[1024,2,256]{2,0,1:T(8,128)(2,1)}, bf16[1024,2,256]{2,0,1:T(8,128)(2,1)S(1)}, u32[]{:S(2)}, u32[]{:S(2)}) %collective-permute-start) | collective-permute-done | bytes 1048608 | tf_op jit(solution)/shard_map/while/body/eval_jaxpr/ppermute | solution.py:10
  261.7 10.6 %collective-permute-done = bf16[1024,2,256]{2,0,1:T(8,128)(2,1)S(1)} collective-permute-done((bf16[1024,2,256]{2,0,1:T(8,128)(2,1)}, bf16[1024,2,256]{2,0,1:T(8,128)(2,1)S(1)}, u32[]{:S(2)}, u32[]{:S(2)}) %collective-permute-start) | collective-permute-done | bytes 1048608 | tf_op jit(solution)/shard_map/while/body/eval_jaxpr/ppermute | solution.py:10
  287.2 10.6 %collective-permute-done = bf16[1024,2,256]{2,0,1:T(8,128)(2,1)S(1)} collective-permute-done((bf16[1024,2,256]{2,0,1:T(8,128)(2,1)}, bf16[1024,2,256]{2,0,1:T(8,128)(2,1)S(1)}, u32[]{:S(2)}, u32[]{:S(2)}) %collective-permute-start) | collective-permute-done | bytes 1048608 | tf_op jit(solution)/shard_map/while/body/eval_jaxpr/ppermute | solution.py:10
  312.7 10.6 %collective-permute-done = bf16[1024,2,256]{2,0,1:T(8,128)(2,1)S(1)} collective-permute-done((bf16[1024,2,256]{2,0,1:T(8,128)(2,1)}, bf16[1024,2,256]{2,0,1:T(8,128)(2,1)S(1)}, u32[]{:S(2)}, u32[]{:S(2)}) %collective-permute-start) | collective-permute-done | bytes 1048608 | tf_op jit(solution)/shard_map/while/body/eval_jaxpr/ppermute | solution.py:10
  338.2 10.9 %collective-permute-done = bf16[1024,2,256]{2,0,1:T(8,128)(2,1)S(1)} collective-permute-done((bf16[1024,2,256]{2,0,1:T(8,128)(2,1)}, bf16[1024,2,256]{2,0,1:T(8,128)(2,1)S(1)}, u32[]{:S(2)}, u32[]{:S(2)}) %collective-permute-start) | collective-permute-done | bytes 1048608 | tf_op jit(solution)/shard_map/while/body/eval_jaxpr/ppermute | solution.py:10
  351.1 4.9 conditional.2
  367.6 10.6 %collective-permute-done = bf16[1024,2,256]{2,0,1:T(8,128)(2,1)S(1)} collective-permute-done((bf16[1024,2,256]{2,0,1:T(8,128)(2,1)}, bf16[1024,2,256]{2,0,1:T(8,128)(2,1)S(1)}, u32[]{:S(2)}, u32[]{:S(2)}) %collective-permute-start) | collective-permute-done | bytes 1048608 | tf_op jit(solution)/shard_map/while/body/eval_jaxpr/ppermute | solution.py:10
  380.1 4.9 conditional.2
  381.5 2.3 convolution_convert_fusion
  396.7 10.6 %collective-permute-done = bf16[1024,2,256]{2,0,1:T(8,128)(2,1)S(1)} collective-permute-done((bf16[1024,2,256]{2,0,1:T(8,128)(2,1)}, bf16[1024,2,256]{2,0,1:T(8,128)(2,1)S(1)}, u32[]{:S(2)}, u32[]{:S(2)}) %collective-permute-start) | collective-permute-done | bytes 1048608 | tf_op jit(solution)/shard_map/while/body/eval_jaxpr/ppermute | solution.py:10
  409.2 4.9 conditional.2
  425.8 10.6 %collective-permute-done = bf16[1024,2,256]{2,0,1:T(8,128)(2,1)S(1)} collective-permute-done((bf16[1024,2,256]{2,0,1:T(8,128)(2,1)}, bf16[1024,2,256]{2,0,1:T(8,128)(2,1)S(1)}, u32[]{:S(2)}, u32[]{:S(2)}) %collective-permute-start) | collective-permute-done | bytes 1048608 | tf_op jit(solution)/shard_map/while/body/eval_jaxpr/ppermute | solution.py:10
  438.3 4.9 conditional.2
  454.9 10.6 %collective-permute-done = bf16[1024,2,256]{2,0,1:T(8,128)(2,1)S(1)} collective-permute-done((bf16[1024,2,256]{2,0,1:T(8,128)(2,1)}, bf16[1024,2,256]{2,0,1:T(8,128)(2,1)S(1)}, u32[]{:S(2)}, u32[]{:S(2)}) %collective-permute-start) | collective-permute-done | bytes 1048608 | tf_op jit(solution)/shard_map/while/body/eval_jaxpr/ppermute | solution.py:10
  467.4 4.9 conditional.2
  484.0 10.6 %collective-permute-done = bf16[1024,2,256]{2,0,1:T(8,128)(2,1)S(1)} collective-permute-done((bf16[1024,2,256]{2,0,1:T(8,128)(2,1)}, bf16[1024,2,256]{2,0,1:T(8,128)(2,1)S(1)}, u32[]{:S(2)}, u32[]{:S(2)}) %collective-permute-start) | collective-permute-done | bytes 1048608 | tf_op jit(solution)/shard_map/while/body/eval_jaxpr/ppermute | solution.py:10
  496.5 4.9 conditional.2
  513.1 10.6 %collective-permute-done = bf16[1024,2,256]{2,0,1:T(8,128)(2,1)S(1)} collective-permute-done((bf16[1024,2,256]{2,0,1:T(8,128)(2,1)}, bf16[1024,2,256]{2,0,1:T(8,128)(2,1)S(1)}, u32[]{:S(2)}, u32[]{:S(2)}) %collective-permute-start) | collective-permute-done | bytes 1048608 | tf_op jit(solution)/shard_map/while/body/eval_jaxpr/ppermute | solution.py:10
  538.6 10.6 %collective-permute-done = bf16[1024,2,256]{2,0,1:T(8,128)(2,1)S(1)} collective-permute-done((bf16[1024,2,256]{2,0,1:T(8,128)(2,1)}, bf16[1024,2,256]{2,0,1:T(8,128)(2,1)S(1)}, u32[]{:S(2)}, u32[]{:S(2)}) %collective-permute-start) | collective-permute-done | bytes 1048608 | tf_op jit(solution)/shard_map/while/body/eval_jaxpr/ppermute | solution.py:10
  564.1 10.6 %collective-permute-done = bf16[1024,2,256]{2,0,1:T(8,128)(2,1)S(1)} collective-permute-done((bf16[1024,2,256]{2,0,1:T(8,128)(2,1)}, bf16[1024,2,256]{2,0,1:T(8,128)(2,1)S(1)}, u32[]{:S(2)}, u32[]{:S(2)}) %collective-permute-start) | collective-permute-done | bytes 1048608 | tf_op jit(solution)/shard_map/while/body/eval_jaxpr/ppermute | solution.py:10
  580.6 134.3 %all_to_all.20 = bf16[6,1024,2,256]{3,2,0,1:T(2,128)(2,1)S(1)} all-to-all(bf16[6,1024,2,256]{3,2,0,1:T(2,128)(2,1)} %get-tuple-element.205), channel_id=1, replica_groups=mesh['sec'=8,'ch'=4] {'ch'}, dimensions={1} | all-to-all | bytes 12582912 | tf_op jit(solution)/shard_map/all_to_all | solution.py:69
  714.9 10.7 %copy.22 = bf16[6,256,2,4,256]{4,3,2,1,0:T(4,128)(2,1)} copy(bf16[6,256,2,4,256]{4,2,0,1,3:T(2,128)(2,1)S(1)} %bitcast.33) | data formatting | bytes 12582912 | tf_op jit(solution)/shard_map/all_to_all | solution.py:69
  725.7 11.0 %broadcast_in_dim_reshape.3 = bf16[1,6,256,2048]{3,2,1,0:T(8,128)(2,1)} reshape(bf16[6,256,2,4,256]{4,3,2,1,0:T(4,128)(2,1)} %copy.22) | data formatting | bytes 12582912 | tf_op jit(solution)/shard_map/broadcast_in_dim;reshape | solution.py:70
  (235 shorter events, 222.8 us)
Async XLA Ops:
  36.1 6.1 copy-start
  36.1 177.6 %all-to-all-start = ((bf16[4,6,256,2,256]{4,3,2,1,0:T(2,128)(2,1)}), bf16[4,6,256,2,256]{4,3,2,1,0:T(2,128)(2,1)}, u32[]{:S(2)}, u32[]{:S(2)}) async-start(bf16[4,6,256,2,256]{4,3,2,1,0:T(2,128)(2,1)} %pad_maximum_fusion.1), calls=%async_computation | async-start | bytes 12582912 | tf_op jit(solution)/shard_map/all_to_all | solution.py:32
  41.4 178.8 %all-gather.2.cloned.1.call-start = ((), (), s32[]{:S(2)}) async-start(), calls=%async_computation.2 | async-start | bytes 2621440 | tf_op jit(solution)/shard_map/all_gather | solution.py:24
  220.2 7.1 copy-start.2
  229.6 17.2 %collective-permute-start = (bf16[1024,2,256]{2,0,1:T(8,128)(2,1)}, bf16[1024,2,256]{2,0,1:T(8,128)(2,1)S(1)}, u32[]{:S(2)}, u32[]{:S(2)}) collective-permute-start(bf16[1024,2,256]{2,0,1:T(8,128)(2,1)} %copy.31), channel_id=1, source_target_pairs={{0,4},{4,8},{8,12},{12,16},{16,20},{20,24},{24,28},{1,5},{5,9},{9,... | collective-permute-start | bytes 3145736 | tf_op jit(solution)/shard_map/while/body/eval_jaxpr/ppermute | solution.py:10
  235.5 13.3 %copy-start.1 = (bf16[1024,1024]{1,0:T(8,128)(2,1)S(1)}, bf16[1024,1024]{1,0:T(8,128)(2,1)}, u32[]{:S(2)}) copy-start(bf16[1024,1024]{1,0:T(8,128)(2,1)} %get-tuple-element.351) | copy-start | bytes 6291460 | tf_op jit(solution)/shard_map/while
  255.1 17.2 %collective-permute-start = (bf16[1024,2,256]{2,0,1:T(8,128)(2,1)}, bf16[1024,2,256]{2,0,1:T(8,128)(2,1)S(1)}, u32[]{:S(2)}, u32[]{:S(2)}) collective-permute-start(bf16[1024,2,256]{2,0,1:T(8,128)(2,1)} %copy.31), channel_id=1, source_target_pairs={{0,4},{4,8},{8,12},{12,16},{16,20},{20,24},{24,28},{1,5},{5,9},{9,... | collective-permute-start | bytes 3145736 | tf_op jit(solution)/shard_map/while/body/eval_jaxpr/ppermute | solution.py:10
  261.0 13.3 %copy-start.1 = (bf16[1024,1024]{1,0:T(8,128)(2,1)S(1)}, bf16[1024,1024]{1,0:T(8,128)(2,1)}, u32[]{:S(2)}) copy-start(bf16[1024,1024]{1,0:T(8,128)(2,1)} %get-tuple-element.351) | copy-start | bytes 6291460 | tf_op jit(solution)/shard_map/while
  280.6 17.2 %collective-permute-start = (bf16[1024,2,256]{2,0,1:T(8,128)(2,1)}, bf16[1024,2,256]{2,0,1:T(8,128)(2,1)S(1)}, u32[]{:S(2)}, u32[]{:S(2)}) collective-permute-start(bf16[1024,2,256]{2,0,1:T(8,128)(2,1)} %copy.31), channel_id=1, source_target_pairs={{0,4},{4,8},{8,12},{12,16},{16,20},{20,24},{24,28},{1,5},{5,9},{9,... | collective-permute-start | bytes 3145736 | tf_op jit(solution)/shard_map/while/body/eval_jaxpr/ppermute | solution.py:10
  286.5 13.3 %copy-start.1 = (bf16[1024,1024]{1,0:T(8,128)(2,1)S(1)}, bf16[1024,1024]{1,0:T(8,128)(2,1)}, u32[]{:S(2)}) copy-start(bf16[1024,1024]{1,0:T(8,128)(2,1)} %get-tuple-element.351) | copy-start | bytes 6291460 | tf_op jit(solution)/shard_map/while
  306.0 17.2 %collective-permute-start = (bf16[1024,2,256]{2,0,1:T(8,128)(2,1)}, bf16[1024,2,256]{2,0,1:T(8,128)(2,1)S(1)}, u32[]{:S(2)}, u32[]{:S(2)}) collective-permute-start(bf16[1024,2,256]{2,0,1:T(8,128)(2,1)} %copy.31), channel_id=1, source_target_pairs={{0,4},{4,8},{8,12},{12,16},{16,20},{20,24},{24,28},{1,5},{5,9},{9,... | collective-permute-start | bytes 3145736 | tf_op jit(solution)/shard_map/while/body/eval_jaxpr/ppermute | solution.py:10
  311.9 13.3 %copy-start.1 = (bf16[1024,1024]{1,0:T(8,128)(2,1)S(1)}, bf16[1024,1024]{1,0:T(8,128)(2,1)}, u32[]{:S(2)}) copy-start(bf16[1024,1024]{1,0:T(8,128)(2,1)} %get-tuple-element.351) | copy-start | bytes 6291460 | tf_op jit(solution)/shard_map/while
  331.5 17.6 %collective-permute-start = (bf16[1024,2,256]{2,0,1:T(8,128)(2,1)}, bf16[1024,2,256]{2,0,1:T(8,128)(2,1)S(1)}, u32[]{:S(2)}, u32[]{:S(2)}) collective-permute-start(bf16[1024,2,256]{2,0,1:T(8,128)(2,1)} %copy.31), channel_id=1, source_target_pairs={{0,4},{4,8},{8,12},{12,16},{16,20},{20,24},{24,28},{1,5},{5,9},{9,... | collective-permute-start | bytes 3145736 | tf_op jit(solution)/shard_map/while/body/eval_jaxpr/ppermute | solution.py:10
  337.4 13.6 %copy-start.1 = (bf16[1024,1024]{1,0:T(8,128)(2,1)S(1)}, bf16[1024,1024]{1,0:T(8,128)(2,1)}, u32[]{:S(2)}) copy-start(bf16[1024,1024]{1,0:T(8,128)(2,1)} %get-tuple-element.351) | copy-start | bytes 6291460 | tf_op jit(solution)/shard_map/while
  361.0 17.2 %collective-permute-start = (bf16[1024,2,256]{2,0,1:T(8,128)(2,1)}, bf16[1024,2,256]{2,0,1:T(8,128)(2,1)S(1)}, u32[]{:S(2)}, u32[]{:S(2)}) collective-permute-start(bf16[1024,2,256]{2,0,1:T(8,128)(2,1)} %copy.31), channel_id=1, source_target_pairs={{0,4},{4,8},{8,12},{12,16},{16,20},{20,24},{24,28},{1,5},{5,9},{9,... | collective-permute-start | bytes 3145736 | tf_op jit(solution)/shard_map/while/body/eval_jaxpr/ppermute | solution.py:10
  366.9 13.3 %copy-start.1 = (bf16[1024,1024]{1,0:T(8,128)(2,1)S(1)}, bf16[1024,1024]{1,0:T(8,128)(2,1)}, u32[]{:S(2)}) copy-start(bf16[1024,1024]{1,0:T(8,128)(2,1)} %get-tuple-element.351) | copy-start | bytes 6291460 | tf_op jit(solution)/shard_map/while
  390.1 17.2 %collective-permute-start = (bf16[1024,2,256]{2,0,1:T(8,128)(2,1)}, bf16[1024,2,256]{2,0,1:T(8,128)(2,1)S(1)}, u32[]{:S(2)}, u32[]{:S(2)}) collective-permute-start(bf16[1024,2,256]{2,0,1:T(8,128)(2,1)} %copy.31), channel_id=1, source_target_pairs={{0,4},{4,8},{8,12},{12,16},{16,20},{20,24},{24,28},{1,5},{5,9},{9,... | collective-permute-start | bytes 3145736 | tf_op jit(solution)/shard_map/while/body/eval_jaxpr/ppermute | solution.py:10
  396.0 13.3 %copy-start.1 = (bf16[1024,1024]{1,0:T(8,128)(2,1)S(1)}, bf16[1024,1024]{1,0:T(8,128)(2,1)}, u32[]{:S(2)}) copy-start(bf16[1024,1024]{1,0:T(8,128)(2,1)} %get-tuple-element.351) | copy-start | bytes 6291460 | tf_op jit(solution)/shard_map/while
  419.2 17.2 %collective-permute-start = (bf16[1024,2,256]{2,0,1:T(8,128)(2,1)}, bf16[1024,2,256]{2,0,1:T(8,128)(2,1)S(1)}, u32[]{:S(2)}, u32[]{:S(2)}) collective-permute-start(bf16[1024,2,256]{2,0,1:T(8,128)(2,1)} %copy.31), channel_id=1, source_target_pairs={{0,4},{4,8},{8,12},{12,16},{16,20},{20,24},{24,28},{1,5},{5,9},{9,... | collective-permute-start | bytes 3145736 | tf_op jit(solution)/shard_map/while/body/eval_jaxpr/ppermute | solution.py:10
  425.1 13.3 %copy-start.1 = (bf16[1024,1024]{1,0:T(8,128)(2,1)S(1)}, bf16[1024,1024]{1,0:T(8,128)(2,1)}, u32[]{:S(2)}) copy-start(bf16[1024,1024]{1,0:T(8,128)(2,1)} %get-tuple-element.351) | copy-start | bytes 6291460 | tf_op jit(solution)/shard_map/while
  448.3 17.2 %collective-permute-start = (bf16[1024,2,256]{2,0,1:T(8,128)(2,1)}, bf16[1024,2,256]{2,0,1:T(8,128)(2,1)S(1)}, u32[]{:S(2)}, u32[]{:S(2)}) collective-permute-start(bf16[1024,2,256]{2,0,1:T(8,128)(2,1)} %copy.31), channel_id=1, source_target_pairs={{0,4},{4,8},{8,12},{12,16},{16,20},{20,24},{24,28},{1,5},{5,9},{9,... | collective-permute-start | bytes 3145736 | tf_op jit(solution)/shard_map/while/body/eval_jaxpr/ppermute | solution.py:10
  454.2 13.3 %copy-start.1 = (bf16[1024,1024]{1,0:T(8,128)(2,1)S(1)}, bf16[1024,1024]{1,0:T(8,128)(2,1)}, u32[]{:S(2)}) copy-start(bf16[1024,1024]{1,0:T(8,128)(2,1)} %get-tuple-element.351) | copy-start | bytes 6291460 | tf_op jit(solution)/shard_map/while
  477.3 17.2 %collective-permute-start = (bf16[1024,2,256]{2,0,1:T(8,128)(2,1)}, bf16[1024,2,256]{2,0,1:T(8,128)(2,1)S(1)}, u32[]{:S(2)}, u32[]{:S(2)}) collective-permute-start(bf16[1024,2,256]{2,0,1:T(8,128)(2,1)} %copy.31), channel_id=1, source_target_pairs={{0,4},{4,8},{8,12},{12,16},{16,20},{20,24},{24,28},{1,5},{5,9},{9,... | collective-permute-start | bytes 3145736 | tf_op jit(solution)/shard_map/while/body/eval_jaxpr/ppermute | solution.py:10
  483.2 13.3 %copy-start.1 = (bf16[1024,1024]{1,0:T(8,128)(2,1)S(1)}, bf16[1024,1024]{1,0:T(8,128)(2,1)}, u32[]{:S(2)}) copy-start(bf16[1024,1024]{1,0:T(8,128)(2,1)} %get-tuple-element.351) | copy-start | bytes 6291460 | tf_op jit(solution)/shard_map/while
  506.4 17.2 %collective-permute-start = (bf16[1024,2,256]{2,0,1:T(8,128)(2,1)}, bf16[1024,2,256]{2,0,1:T(8,128)(2,1)S(1)}, u32[]{:S(2)}, u32[]{:S(2)}) collective-permute-start(bf16[1024,2,256]{2,0,1:T(8,128)(2,1)} %copy.31), channel_id=1, source_target_pairs={{0,4},{4,8},{8,12},{12,16},{16,20},{20,24},{24,28},{1,5},{5,9},{9,... | collective-permute-start | bytes 3145736 | tf_op jit(solution)/shard_map/while/body/eval_jaxpr/ppermute | solution.py:10
  512.3 13.3 %copy-start.1 = (bf16[1024,1024]{1,0:T(8,128)(2,1)S(1)}, bf16[1024,1024]{1,0:T(8,128)(2,1)}, u32[]{:S(2)}) copy-start(bf16[1024,1024]{1,0:T(8,128)(2,1)} %get-tuple-element.351) | copy-start | bytes 6291460 | tf_op jit(solution)/shard_map/while
  531.9 17.2 %collective-permute-start = (bf16[1024,2,256]{2,0,1:T(8,128)(2,1)}, bf16[1024,2,256]{2,0,1:T(8,128)(2,1)S(1)}, u32[]{:S(2)}, u32[]{:S(2)}) collective-permute-start(bf16[1024,2,256]{2,0,1:T(8,128)(2,1)} %copy.31), channel_id=1, source_target_pairs={{0,4},{4,8},{8,12},{12,16},{16,20},{20,24},{24,28},{1,5},{5,9},{9,... | collective-permute-start | bytes 3145736 | tf_op jit(solution)/shard_map/while/body/eval_jaxpr/ppermute | solution.py:10
  537.8 13.3 %copy-start.1 = (bf16[1024,1024]{1,0:T(8,128)(2,1)S(1)}, bf16[1024,1024]{1,0:T(8,128)(2,1)}, u32[]{:S(2)}) copy-start(bf16[1024,1024]{1,0:T(8,128)(2,1)} %get-tuple-element.351) | copy-start | bytes 6291460 | tf_op jit(solution)/shard_map/while
  557.4 17.2 %collective-permute-start = (bf16[1024,2,256]{2,0,1:T(8,128)(2,1)}, bf16[1024,2,256]{2,0,1:T(8,128)(2,1)S(1)}, u32[]{:S(2)}, u32[]{:S(2)}) collective-permute-start(bf16[1024,2,256]{2,0,1:T(8,128)(2,1)} %copy.31), channel_id=1, source_target_pairs={{0,4},{4,8},{8,12},{12,16},{16,20},{20,24},{24,28},{1,5},{5,9},{9,... | collective-permute-start | bytes 3145736 | tf_op jit(solution)/shard_map/while/body/eval_jaxpr/ppermute | solution.py:10
  563.3 13.3 %copy-start.1 = (bf16[1024,1024]{1,0:T(8,128)(2,1)S(1)}, bf16[1024,1024]{1,0:T(8,128)(2,1)}, u32[]{:S(2)}) copy-start(bf16[1024,1024]{1,0:T(8,128)(2,1)} %get-tuple-element.351) | copy-start | bytes 6291460 | tf_op jit(solution)/shard_map/while
Sparse Core Ops, SparseCore 0:
  43.8 86.7 all-gather.1
